TPU v7x, 128 devices: a whole 4x4x4 slice. The times are simulated.
128 devices in a mesh: row: 8 (over z_lo, y), col: 16 (over z_hi, x, core).
Axes of the slice: x: 4, y: 4, z: 4 (z_hi: 2, z_lo: 2; z = z_hi * 2 + z_lo), core: 2. Of those that a mesh axis runs over, the one named last changes fastest.
Arguments:
- slip: float32 [262144, 256], P(('row', 'col')), may hold values from -2 to 2
- state: float32 [262144, 256], P(('row', 'col')), may hold values from 0.4 to 0.9
- tau_load: float32 [262144], P(('row', 'col')), may hold values from 1 to 2
- normal_stress: float32 [262144], P(('row', 'col')), may hold values from 6 to 8
- direct_effect: float32 [262144], P(('row', 'col')), may hold values from 0.8 to 1.6
- evolution_effect: float32 [262144], P(('row', 'col')), may hold values from 0.5 to 1
- slip_distance: float32 [262144], P(('row', 'col')), may hold values from 0.5 to 2
- self_stiffness: float32 [262144], P(('row', 'col')), may hold values from 0.5 to 2
- near_blocks: bfloat16 [3, 262144, 256], P(None, ('row', 'col')), may hold values from -0.21875 to 0.21875
- basis_in: bfloat16 [32, 262144], P(None, ('row', 'col')), may hold values from -0.375 to 0.375
- basis_out: bfloat16 [32, 262144], P(None, ('row', 'col')), may hold values from -1 to 1
- coupling: bfloat16 [32768, 8, 4096], P('row', None, 'col'), may hold values from -0.046875 to 0.046875
- block_rank: int32 [1024, 8, 128], P('row', None, 'col'), may hold values from 8 to 32
- adj_bricks: int32 [8, 262144], P(None, ('row', 'col')), may hold values from 0 to 2047
- adj_count: int32 [262144], P(('row', 'col')), may hold values from 1 to 8
- adj_weight: float32 [8, 262144], P(None, ('row', 'col')), may hold values from 0.05 to 1
- pressure_now: bfloat16 [2048, 256], P('col'), may hold values from 0.099609375 to 1
- pressure_rate: bfloat16 [2048, 256], P('col'), may hold values from 0.5 to 5
Outputs:
- slip_out: float32 [262144, 256], P(('row', 'col'))
- state_out: float32 [262144, 256], P(('row', 'col'))
Inputs may be any that keep to these rules, and one draw needn't show every extreme that they name: Only the first adj_count entries of a patch's brick list are read. `adj_bricks`: brick numbers index the whole reservoir. `block_rank`: ranks of pairs with |i - j| <= 1 are not read.
All inputs are finite; a program needn't handle non-finite values.
Results may differ from a plain program's by a relative error of at most 0.0007.
Values may be sent and summed in bfloat16 or wider, within the bound.
A program may use at most 192 MiB of HBM per device.

v0:
```python
import jax
import jax.numpy as jnp
from jax import lax
from jax.sharding import PartitionSpec as P

BS = 256
R = 32
BPD = 8
STEP_SIZE = 0.5
REF_FRICTION = 0.6


def with_halo(array, sides, width):
    for axis, dim in sides:
        devices, length = (lax.axis_size(axis), array.shape[dim])
        up = [(i, (i + 1) % devices) for i in range(devices - 1)]
        down = [(j, i) for i, j in up]
        last = lax.slice_in_dim(array, length - width, length, axis=dim)
        initial = lax.slice_in_dim(array, 0, width, axis=dim)
        before = lax.ppermute(last, axis, up)
        after = lax.ppermute(initial, axis, down)
        array = jnp.concatenate([before, array, after], axis=dim)
    return array


def fault_pressure(joined, adj_bricks, adj_count, adj_weight):
    slots = adj_bricks.shape[0]
    patches = adj_bricks.shape[1]
    slot_ids = jnp.arange(slots, dtype=jnp.int32)
    live = (adj_count[None, :] > slot_ids[:, None]).astype(jnp.float32)
    weighting = adj_weight * live
    weight_sum = jnp.sum(weighting, axis=0)
    picked = joined[adj_bricks.reshape(slots * patches)].reshape(slots, patches, joined.shape[1])
    total = jnp.sum(weighting[:, :, None] * picked.astype(jnp.float32), axis=0)
    return total / weight_sum[:, None]


def far_mask_flat(row_blocks, col_blocks, ranks):
    row_total = row_blocks.shape[0]
    col_total = col_blocks.shape[0]
    row_block_of = jnp.repeat(row_blocks, R)
    col_block_of = jnp.repeat(col_blocks, R)
    row_level = jnp.arange(row_total * R, dtype=jnp.int32) % R
    col_level = jnp.arange(col_total * R, dtype=jnp.int32) % R
    spread = (
        jnp.arange(col_total, dtype=jnp.int32)[:, None]
        == (jnp.arange(col_total * R, dtype=jnp.int32) // R)[None, :]
    ).astype(jnp.float32)
    rank_cols = jnp.dot(
        ranks.astype(jnp.float32),
        spread,
        precision=lax.Precision.HIGHEST,
        preferred_element_type=jnp.float32,
    )
    rank_full = jnp.broadcast_to(rank_cols[:, None, :], (row_total, R, col_total * R)).reshape(
        row_total * R, col_total * R
    )
    level = jnp.maximum(row_level[:, None], col_level[None, :]).astype(jnp.float32)
    apart = jnp.abs(row_block_of[:, None] - col_block_of[None, :]) > 1
    return apart & (level < rank_full)


def rates(
    slip_now,
    state_now,
    outer,
    pressure,
    tau_load,
    normal_stress,
    direct_effect,
    evolution_effect,
    slip_distance,
    self_stiffness,
):
    tau = tau_load[:, None] - self_stiffness[:, None] * slip_now - outer
    sigma = normal_stress[:, None] - pressure
    speed = jnp.exp((tau / sigma - state_now) / direct_effect[:, None])
    drift = (evolution_effect / slip_distance)[:, None] * (
        jnp.exp((REF_FRICTION - state_now) / evolution_effect[:, None]) - speed
    )
    return (speed, drift)


def project(basis, slips):
    count = slips.shape[0] // BS
    coeff = jnp.einsum(
        "rnb,nbe->nre",
        basis.reshape(R, count, BS),
        slips.reshape(count, BS, slips.shape[1]),
        preferred_element_type=jnp.float32,
    )
    return coeff.astype(jnp.bfloat16).reshape(count * R, slips.shape[1])


def near_field(padded, near_blocks):
    patches = near_blocks.shape[1]
    count = patches // BS
    terms = []
    for neighbour in range(3):
        window = padded[neighbour * BS : neighbour * BS + patches].reshape(
            count, BS, padded.shape[1]
        )
        terms.append(
            jnp.einsum(
                "gns,gsl->gnl",
                near_blocks[neighbour].reshape(count, BS, BS),
                window,
                preferred_element_type=jnp.float32,
            )
        )
    return (terms[0] + terms[1] + terms[2]).reshape(patches, padded.shape[1])


def per_device(
    slip,
    state,
    tau_load,
    normal_stress,
    direct_effect,
    evolution_effect,
    slip_distance,
    self_stiffness,
    near_blocks,
    basis_in,
    basis_out,
    coupling,
    block_rank,
    adj_bricks,
    adj_count,
    adj_weight,
    pressure_now,
    pressure_rate,
):
    now_all, rate_all = (
        lax.all_gather(pressure_now, "col", axis=0, tiled=True),
        lax.all_gather(pressure_rate, "col", axis=0, tiled=True),
    )
    scenarios = slip.shape[1]
    joined = jnp.concatenate([now_all, rate_all], 1)
    both_press = fault_pressure(joined, adj_bricks, adj_count, adj_weight)
    base_press = both_press[:, :scenarios]
    rate_press = both_press[:, scenarios:]
    row_count = lax.axis_size("row")
    col_count = lax.axis_size("col")
    row_index = lax.axis_index("row")
    col_index = lax.axis_index("col")
    matrix = coupling.reshape(coupling.shape[0], coupling.shape[1] * coupling.shape[2])
    ranks = block_rank.reshape(block_rank.shape[0], block_rank.shape[1] * block_rank.shape[2])
    row_blocks = row_index * (col_count * BPD) + jnp.arange(col_count * BPD, dtype=jnp.int32)
    source_rows = jnp.arange(row_count, dtype=jnp.int32)[:, None] * col_count + col_index
    col_blocks = (source_rows * BPD + jnp.arange(BPD, dtype=jnp.int32)[None, :]).reshape(
        row_count * BPD
    )
    keep = far_mask_flat(row_blocks, col_blocks, ranks)
    masked = jnp.where(keep, matrix, jnp.zeros((), jnp.bfloat16))
    share = BPD * R
    basis_all = lax.all_gather(basis_in, "row", axis=1, tiled=True)

    def stress(slip_now):
        rounded = slip_now.astype(jnp.bfloat16)
        slip_all = lax.all_gather(rounded, "row", axis=0, tiled=True)
        coeff = project(basis_all, slip_all)
        partial_sum = jnp.dot(masked, coeff, preferred_element_type=jnp.float32)
        total = lax.psum(partial_sum.astype(jnp.bfloat16), "col").astype(jnp.float32)
        mine = lax.dynamic_slice_in_dim(total, col_index * share, share, 0)
        far_coeff = mine.astype(jnp.bfloat16)
        far = jnp.einsum(
            "rnb,nre->nbe",
            basis_out.reshape(R, BPD, BS),
            far_coeff.reshape(BPD, R, slip_now.shape[1]),
            preferred_element_type=jnp.float32,
        )
        far = far.reshape(slip_now.shape)
        padded = with_halo(rounded, ((("row", "col"), 0),), BS)
        near = near_field(padded, near_blocks)
        return near + far

    params = (
        tau_load,
        normal_stress,
        direct_effect,
        evolution_effect,
        slip_distance,
        self_stiffness,
    )
    speed0, drift0 = rates(slip, state, stress(slip), base_press, *params)
    slip_mid = slip + STEP_SIZE * speed0
    state_mid = state + STEP_SIZE * drift0
    speed1, drift1 = rates(
        slip_mid, state_mid, stress(slip_mid), base_press + STEP_SIZE * rate_press, *params
    )
    slip_out = slip + 0.5 * STEP_SIZE * (speed0 + speed1)
    state_out = state + 0.5 * STEP_SIZE * (drift0 + drift1)
    return (slip_out, state_out)


def solution(mesh):
    in_specs = (
        P(("row", "col"), None),
        P(("row", "col"), None),
        P(("row", "col")),
        P(("row", "col")),
        P(("row", "col")),
        P(("row", "col")),
        P(("row", "col")),
        P(("row", "col")),
        P(None, ("row", "col"), None),
        P(None, ("row", "col")),
        P(None, ("row", "col")),
        P("row", None, "col"),
        P("row", None, "col"),
        P(None, ("row", "col")),
        P(("row", "col")),
        P(None, ("row", "col")),
        P("col", None),
        P("col", None),
    )
    out_specs = (P(("row", "col"), None), P(("row", "col"), None))
    return jax.shard_map(
        per_device, mesh=mesh, in_specs=in_specs, out_specs=out_specs, check_vma=False
    )
```

profile of v0, /device:TPU:1, one launch (start us, length us, event | category | flops | bytes accessed | tf_op | source)
XLA Modules:
  0.0 662.5 jit_solution(3476036359275173559)
XLA Ops:
  8.0 2.7 convert_element_type.52
  12.4 4.5 collective-permute-start
  16.9 1.9 collective-permute-start.1
  20.7 11.4 %broadcast_in_dim.14 = f32[128,32,2048]{2,1,0:T(8,128)} broadcast(f32[128,2048]{1,0:T(8,128)S(1)} %copy.23), dimensions={0,2} | broadcast | bytes 34603008 | tf_op jit(solution)/shard_map/broadcast_in_dim | solution.py:55
  32.1 19.9 %copy.30 = f32[512,8,8,256]{3,2,1,0:T(8,128)S(1)} copy(f32[512,8,8,256]{3,1,2,0:T(8,128)} %bitcast.99) | data formatting | bytes 67108864
  52.1 22.4 %fusion.2 = bf16[4096,8,256]{2,1,0:T(8,128)(2,1)} fusion(bf16[4096,8,256]{2,1,0:T(8,128)(2,1)} %param.29, f32[512,8,8,256]{3,2,1,0:T(8,128)S(1)} %copy.30, s32[8,256]{1,0:T(8,128)S(1)} %add_select_fusion.2, s32[4096]{0:T(1024)S(1)} %add_select_fusion, s32[8,256]{1,0:T(8,128)S(1)} %broadcast_in_dim.13, s32[4096]{0:T(1024)S(1)} %sub.77), kind=kLoop, calls=%fused_computation.6 | loop fusion | flops 67108864 | bytes 67158016 | tf_op jit(solution)/shard_map/jit(_where)/select_n | solution.py:155
  74.5 16.5 %copy.31 = bf16[512,8,8,256]{3,1,2,0:T(8,128)(2,1)} copy(bf16[512,8,8,256]{3,2,1,0:T(8,128)(2,1)} %bitcast.101) | data formatting | bytes 33554432
  92.5 3.4 fusion.44
  96.0 2.1 pad_maximum_fusion.3
  98.0 1.8 fusion.45
  99.9 45.0 %all-gather.8.cloned.1.call-done = bf16[16384,256]{1,0:T(8,128)(2,1)} async-done(((bf16[2048,256]{1,0:T(8,128)(2,1)}), bf16[16384,256]{1,0:T(8,128)(2,1)}) %all-gather.8.cloned.1.call-update) | async-done | bytes 8388624 | tf_op jit(solution)/shard_map/all_gather | solution.py:161
  144.8 5.2 convolution_convert_fusion.3
  150.0 9.6 %convolution_convert_fusion.1 = bf16[4096,256]{1,0:T(8,128)(2,1)} fusion(bf16[4096,2048]{1,0:T(8,128)(2,1)} %bitcast.106, bf16[2048,256]{1,0:T(8,128)(2,1)S(1)} %bitcast.121), kind=kOutput, calls=%fused_computation.8 | convolution fusion | flops 4296015872 | bytes 19922944 | tf_op jit(solution)/shard_map/dot_general | solution.py:163
  159.9 31.6 %all-gather.10.cloned.1.call-done = bf16[2048,256]{1,0:T(8,128)(2,1)} async-done(((bf16[128,256]{1,0:T(8,128)(2,1)}), bf16[2048,256]{1,0:T(8,128)(2,1)}) %all-gather.10.cloned.1.call-update) | async-done | bytes 1048592 | tf_op jit(solution)/shard_map/all_gather | solution.py:135
  191.5 45.9 %all-gather.12.cloned.1.call-done = bf16[2048,256]{1,0:T(8,128)(2,1)} async-done(((bf16[128,256]{1,0:T(8,128)(2,1)}), bf16[2048,256]{1,0:T(8,128)(2,1)}) %all-gather.12.cloned.1.call-update) | async-done | bytes 1048592 | tf_op jit(solution)/shard_map/all_gather | solution.py:136
  239.1 66.4 %gather_fusion = bf16[16384,512]{1,0:T(8,128)(2,1)} fusion(bf16[2048,512]{1,0:T(8,128)(2,1)S(1)} %pad_maximum_fusion, s32[16384]{0:T(1024)S(1)} %broadcast_clamp_fusion), kind=kCustom, calls=%fused_computation | custom fusion | bytes 33619968 | tf_op jit(solution)/shard_map/gather | solution.py:33
  305.5 7.5 %fusion = f32[2048,512]{1,0:T(8,128)S(1)} fusion(bf16[8,2048,512]{2,1,0:T(8,128)(2,1)} %bitcast.100, f32[8,2048]{1,0:T(8,128)S(1)} %get-tuple-element.7), kind=kLoop, calls=%fused_computation.3 | loop fusion | flops 24117248 | bytes 21037056 | tf_op jit(solution)/shard_map/reduce_sum | solution.py:34
  313.1 2.4 broadcast_divide_fusion
  315.5 67.4 %all-reduce.3.cloned.1.call-done = bf16[4096,256]{1,0:T(8,128)(2,1)} async-done(((bf16[4096,256]{1,0:T(8,128)(2,1)}), bf16[4096,256]{1,0:T(8,128)(2,1)}) %all-reduce.3.cloned.1.call-update) | async-done | bytes 2097168 | tf_op jit(solution)/shard_map/psum | solution.py:164
  384.6 2.8 bitcast_add_fusion
  388.9 3.4 fusion.15
  392.4 93.1 %all-gather.14.cloned.1.call-done = bf16[16384,256]{1,0:T(8,128)(2,1)} async-done(((bf16[2048,256]{1,0:T(8,128)(2,1)}), bf16[16384,256]{1,0:T(8,128)(2,1)}) %all-gather.14.cloned.1.call-update) | async-done | bytes 8388624 | tf_op jit(solution)/shard_map/all_gather | solution.py:161
  485.5 4.8 convolution_convert_fusion.2
  490.3 9.7 %convolution_convert_fusion = bf16[4096,256]{1,0:T(8,128)(2,1)} fusion(bf16[4096,2048]{1,0:T(8,128)(2,1)} %bitcast.107, bf16[2048,256]{1,0:T(8,128)(2,1)S(1)} %bitcast.120), kind=kOutput, calls=%fused_computation.7 | convolution fusion | flops 4296015872 | bytes 19922944 | tf_op jit(solution)/shard_map/dot_general | solution.py:163
  501.2 3.8 collective-permute-start.2
  505.1 1.9 collective-permute-start.3
  507.0 3.1 fusion.47
  510.1 2.6 collective-permute-done.3
  513.7 1.8 fusion.46
  515.5 127.8 %all-reduce.5.cloned.1.call-done = bf16[4096,256]{1,0:T(8,128)(2,1)} async-done(((bf16[4096,256]{1,0:T(8,128)(2,1)}), bf16[4096,256]{1,0:T(8,128)(2,1)}) %all-reduce.5.cloned.1.call-update) | async-done | bytes 2097168 | tf_op jit(solution)/shard_map/psum | solution.py:164
  644.9 2.9 add_add_fusion
  649.6 4.3 multiply_add_fusion
  (99 shorter events, 18.5 us)
Async XLA Ops:
  7.2 92.7 %all-gather.6.cloned.1.call-start = ((), (), s32[]{:S(2)}) async-start(), calls=%async_computation | async-start | bytes 1179648 | tf_op jit(solution)/shard_map/all_gather | solution.py:157
  7.9 11.5 %copy-start.24 = (s32[128,8,8]{0,2,1:T(8,128)S(1)}, s32[128,8,8]{0,2,1:T(8,128)}, u32[]{:S(2)}) copy-start(s32[128,8,8]{0,2,1:T(8,128)} %param.30) | copy-start | bytes 98308
  7.9 136.9 %all-gather.8.cloned.1.call-start = ((), (), s32[]{:S(2)}) async-start(), calls=%async_computation.1 | async-start | bytes 9437184 | tf_op jit(solution)/shard_map/all_gather | solution.py:161
  10.6 180.9 %all-gather.10.cloned.1.call-start = ((), (), s32[]{:S(2)}) async-start(), calls=%async_computation.3 | async-start | bytes 1114112 | tf_op jit(solution)/shard_map/all_gather | solution.py:135
  11.4 226.0 %all-gather.12.cloned.1.call-start = ((), (), s32[]{:S(2)}) async-start(), calls=%async_computation.4 | async-start | bytes 1114112 | tf_op jit(solution)/shard_map/all_gather | solution.py:136
  12.4 83.5 %collective-permute-start = (bf16[256,256]{1,0:T(8,128)(2,1)S(1)}, bf16[256,256]{1,0:T(8,128)(2,1)}, u32[]{:S(2)}, u32[]{:S(2)}) collective-permute-start(bf16[256,256]{1,0:T(8,128)(2,1)S(1)} %get-tuple-element.18), channel_id=1, source_target_pairs={{0,1},{1,2},{2,3},{3,4},{4,5},{5,6},{6,7},{7,8},{8,9},{9,10},{10,1... | collective-permute-start | bytes 393224 | tf_op jit(solution)/shard_map/ppermute | solution.py:20
  16.9 79.0 %collective-permute-start.1 = (bf16[256,256]{1,0:T(8,128)(2,1)S(1)}, bf16[256,256]{1,0:T(8,128)(2,1)}, u32[]{:S(2)}, u32[]{:S(2)}) collective-permute-start(bf16[256,256]{1,0:T(8,128)(2,1)S(1)} %get-tuple-element.17), channel_id=1, source_target_pairs={{1,0},{2,1},{3,2},{4,3},{5,4},{6,5},{7,6},{8,7},{9,8},{10,9},{11,1... | collective-permute-start | bytes 393224 | tf_op jit(solution)/shard_map/ppermute | solution.py:21
  18.9 364.0 %all-reduce.3.cloned.1.call-start = ((), (), s32[]{:S(2)}) async-start(), calls=%async_computation.2 | async-start | bytes 4194304 | tf_op jit(solution)/shard_map/psum | solution.py:164
  74.5 16.5 %copy-start.15 = (bf16[3,2048,256]{2,1,0:T(8,128)(2,1)S(1)}, bf16[3,2048,256]{2,1,0:T(8,128)(2,1)}, u32[]{:S(2)}) copy-start(bf16[3,2048,256]{2,1,0:T(8,128)(2,1)} %param.26) | copy-start | bytes 9437188
  92.1 5.9 copy-start.9
  92.1 292.3 %copy-start.7 = (bf16[1,2048,256]{2,1,0:T(8,128)(2,1)}, bf16[1,2048,256]{2,1,0:T(8,128)(2,1)S(1)}, u32[]{:S(2)}) copy-start(bf16[1,2048,256]{2,1,0:T(8,128)(2,1)S(1)} %get-tuple-element.8) | copy-start | bytes 3145732
  92.5 3.4 copy-start.18
  92.5 3.4 copy-start.25
  159.7 325.8 %all-gather.14.cloned.1.call-start = ((), (), s32[]{:S(2)}) async-start(), calls=%async_computation.5 | async-start | bytes 9437184 | tf_op jit(solution)/shard_map/all_gather | solution.py:161
  313.1 70.9 %copy-start.16 = (bf16[32,2048]{1,0:T(8,128)(2,1)S(1)}, bf16[32,2048]{1,0:T(8,128)(2,1)}, u32[]{:S(2)}) copy-start(bf16[32,2048]{1,0:T(8,128)(2,1)} %param.28) | copy-start | bytes 393220
  382.9 1.7 copy-start.11
  384.5 2.8 copy-start
  384.5 3.8 copy-start.1
  384.5 4.4 copy-start.12
  384.5 4.4 copy-start.20
  384.5 4.4 copy-start.21
  384.6 4.4 copy-start.22
  384.6 4.4 copy-start.23
  392.3 93.1 %copy-start.6 = (bf16[32,16384]{1,0:T(8,128)(2,1)S(1)}, bf16[32,16384]{1,0:T(8,128)(2,1)}, u32[]{:S(2)}) copy-start(bf16[32,16384]{1,0:T(8,128)(2,1)} %all-gather.6.cloned.1.call-done) | copy-start | bytes 3145732
  392.4 251.0 %all-reduce.5.cloned.1.call-start = ((), (), s32[]{:S(2)}) async-start(), calls=%async_computation.6 | async-start | bytes 4194304 | tf_op jit(solution)/shard_map/psum | solution.py:164
  501.2 8.8 %collective-permute-start.2 = (bf16[256,256]{1,0:T(8,128)(2,1)S(1)}, bf16[256,256]{1,0:T(8,128)(2,1)S(1)}, u32[]{:S(2)}, u32[]{:S(2)}) collective-permute-start(bf16[256,256]{1,0:T(8,128)(2,1)S(1)} %get-tuple-element.13), channel_id=1, source_target_pairs={{0,1},{1,2},{2,3},{3,4},{4,5},{5,6},{6,7},{7,8},{8,9},{9,10},{10,1... | collective-permute-start | bytes 393224 | tf_op jit(solution)/shard_map/ppermute | solution.py:20
  505.1 7.6 %collective-permute-start.3 = (bf16[256,256]{1,0:T(8,128)(2,1)S(1)}, bf16[256,256]{1,0:T(8,128)(2,1)S(1)}, u32[]{:S(2)}, u32[]{:S(2)}) collective-permute-start(bf16[256,256]{1,0:T(8,128)(2,1)S(1)} %get-tuple-element.14), channel_id=1, source_target_pairs={{1,0},{2,1},{3,2},{4,3},{5,4},{6,5},{7,6},{8,7},{9,8},{10,9},{11,1... | collective-permute-start | bytes 393224 | tf_op jit(solution)/shard_map/ppermute | solution.py:21
  510.1 3.7 copy-start.10
  515.5 129.3 %copy-start.8 = (bf16[1,2048,256]{2,1,0:T(8,128)(2,1)S(1)}, bf16[1,2048,256]{2,1,0:T(8,128)(2,1)}, u32[]{:S(2)}) copy-start(bf16[1,2048,256]{2,1,0:T(8,128)(2,1)} %copy-done.7) | copy-start | bytes 3145732
  644.8 3.5 copy-start.2
  644.8 4.1 copy-start.5
  644.9 4.7 copy-start.13
  (6 other events, 6.9 us)
Sparse Core Ops, SparseCore 0:
  9.6 36.9 all-gather.5
  48.8 95.9 all-gather.7
  147.3 44.1 all-gather.9
  193.8 43.5 all-gather.11
  240.3 142.5 all-reduce.2
  392.5 92.9 all-gather.13
  500.1 143.1 all-reduce.4
where the time goes:
time: 663 us; the launch traced here: 662 us
  waiting for transfers between devices  415 us (63%)
  local copies, waits for them, and re-layouts  122 us (18%)
  other arithmetic  51.6 us (8%)
  matrix products  47 us (7%)
  between operations  14.5 us (2%)
  starting transfers between devices  12.6 us (2%)
    psum x2, waiting for transfers between devices, stress(): lax.psum(partial_sum.astype(jnp.bfloat16), 'col').astype(jnp.float32)  195 us
    all_gather x2, waiting for transfers between devices, stress(): slip_all = lax.all_gather(rounded, 'row', axis=0, tiled=True)  138 us
    gather x1, local copies, waits for them, and re-layouts, fault_pressure(): joined[adj_bricks.reshape(slots * patches)]  66.4 us
    all_gather x1, waiting for transfers between devices, per_device(): lax.all_gather(pressure_rate, 'col', axis=0, tiled=True)  45.9 us
    unnamed x57, local copies, waits for them, and re-layouts  41.4 us
    all_gather x1, waiting for transfers between devices, per_device(): lax.all_gather(pressure_now, 'col', axis=0, tiled=True)  31.6 us
    select_n x1, other arithmetic, per_device(): masked = jnp.where(keep, matrix, jnp.zeros((), jnp.bfloat16))  22.4 us
    dot_general x2, matrix products, stress(): partial_sum = jnp.dot(masked, coeff, preferred_element_type=jnp.float32)  19.3 us
  transfers between devices with their start and end apart: 11, of which 7 were waited for; matrix products, arithmetic and copies ran while one was open for 28% of the time, Pallas kernels for 0%

commit v1 on v0

--- a/solution.py
+++ b/solution.py
@@ -161,7 +161,9 @@
         slip_all = lax.all_gather(rounded, "row", axis=0, tiled=True)
         coeff = project(basis_all, slip_all)
         partial_sum = jnp.dot(masked, coeff, preferred_element_type=jnp.float32)
-        total = lax.psum(partial_sum.astype(jnp.bfloat16), "col").astype(jnp.float32)
+        total = jnp.sum(lax.all_gather(partial_sum.astype(jnp.bfloat16), "col"), axis=0).astype(
+            jnp.float32
+        )
         mine = lax.dynamic_slice_in_dim(total, col_index * share, share, 0)
         far_coeff = mine.astype(jnp.bfloat16)
         far = jnp.einsum(

time: 663 us -> 770 us (1.16)
  waiting for transfers between devices: 415 us -> 499 us
  other arithmetic: 51.6 us -> 75.2 us
    all_gather x0 -> x2, waiting for transfers between devices: none -> 283 us  [stress(): lax.all_gather(partial_sum.astype(jnp.bfloat16), 'col')]
    psum x2 -> x0, waiting for transfers between devices: 195 us -> none  [stress(): lax.psum(partial_sum.astype(jnp.bfloat16), 'col').astype(jnp.float32)]
    reduce_sum x0 -> x2, other arithmetic: none -> 24.6 us  [stress(): jnp.sum(lax.all_gather(partial_sum.astype(jnp.bfloat16), 'col'), axis=0)]
    all_gather x1, waiting for transfers between devices: 31.6 us -> 17 us  [per_device(): lax.all_gather(pressure_now, 'col', axis=0, tiled=True)]
    all_gather x2, waiting for transfers between devices: 138 us -> 150 us  [stress(): slip_all = lax.all_gather(rounded, 'row', axis=0, tiled=True)]
    unnamed x57 -> x59, local copies, waits for them, and re-layouts: 41.4 us -> 46.4 us
  transfers between devices with their start and end apart: 11 -> 11, of which waited for: 7 -> 7; matrix products, arithmetic and copies ran while one was open for 28% -> 23% of each run, Pallas kernels for 0% -> 0%
where the time goes in v1:
time: 770 us
  waiting for transfers between devices  499 us (65%)
  local copies, waits for them, and re-layouts  127 us (16%)
  other arithmetic  75.2 us (10%)
  matrix products  41.9 us (5%)
  between operations  14.5 us (2%)
  starting transfers between devices  12.2 us (2%)
    all_gather x2, waiting for transfers between devices, stress(): lax.all_gather(partial_sum.astype(jnp.bfloat16), 'col')  283 us
    all_gather x2, waiting for transfers between devices, stress(): slip_all = lax.all_gather(rounded, 'row', axis=0, tiled=True)  150 us
    gather x1, local copies, waits for them, and re-layouts, fault_pressure(): joined[adj_bricks.reshape(slots * patches)]  66.2 us
    unnamed x59, local copies, waits for them, and re-layouts  46.4 us
    all_gather x1, waiting for transfers between devices, per_device(): lax.all_gather(pressure_rate, 'col', axis=0, tiled=True)  45.9 us
    reduce_sum x2, other arithmetic, stress(): jnp.sum(lax.all_gather(partial_sum.astype(jnp.bfloat16), 'col'), axis=0)  24.6 us
    select_n x1, other arithmetic, per_device(): masked = jnp.where(keep, matrix, jnp.zeros((), jnp.bfloat16))  22.4 us
    all_gather x1, waiting for transfers between devices, per_device(): lax.all_gather(pressure_now, 'col', axis=0, tiled=True)  17 us
  transfers between devices with their start and end apart: 11, of which 7 were waited for; matrix products, arithmetic and copies ran while one was open for 23% of the time, Pallas kernels for 0%

profile of v1, /device:TPU:1, one launch (start us, length us, event | category | flops | bytes accessed | tf_op | source)
XLA Modules:
  0.0 769.5 jit_solution(8574325838573936437)
XLA Ops:
  8.0 2.7 convert_element_type.56
  13.8 11.3 %broadcast_in_dim.14 = f32[128,32,2048]{2,1,0:T(8,128)} broadcast(f32[128,2048]{1,0:T(8,128)S(1)} %copy.23), dimensions={0,2} | broadcast | bytes 34603008 | tf_op jit(solution)/shard_map/broadcast_in_dim | solution.py:55
  25.1 19.9 %copy.30 = f32[512,8,8,256]{3,2,1,0:T(8,128)S(1)} copy(f32[512,8,8,256]{3,1,2,0:T(8,128)} %bitcast.101) | data formatting | bytes 67108864
  45.1 22.4 %fusion.2 = bf16[4096,8,256]{2,1,0:T(8,128)(2,1)} fusion(bf16[4096,8,256]{2,1,0:T(8,128)(2,1)} %param.29, f32[512,8,8,256]{3,2,1,0:T(8,128)S(1)} %copy.30, s32[8,256]{1,0:T(8,128)S(1)} %add_select_fusion.2, s32[4096]{0:T(1024)S(1)} %add_select_fusion, s32[8,256]{1,0:T(8,128)S(1)} %broadcast_in_dim.13, s32[4096]{0:T(1024)S(1)} %sub.77), kind=kLoop, calls=%fused_computation.6 | loop fusion | flops 67108864 | bytes 67158016 | tf_op jit(solution)/shard_map/jit(_where)/select_n | solution.py:155
  67.5 16.3 %copy.31 = bf16[512,8,8,256]{3,1,2,0:T(8,128)(2,1)} copy(bf16[512,8,8,256]{3,2,1,0:T(8,128)(2,1)} %bitcast.103) | data formatting | bytes 33554432
  83.9 61.0 %all-gather.12.cloned.1.call-done = bf16[16384,256]{1,0:T(8,128)(2,1)} async-done(((bf16[2048,256]{1,0:T(8,128)(2,1)}), bf16[16384,256]{1,0:T(8,128)(2,1)}) %all-gather.12.cloned.1.call-update) | async-done | bytes 8388624 | tf_op jit(solution)/shard_map/all_gather | solution.py:161
  144.8 5.3 convolution_convert_fusion.3
  150.1 3.2 copy-done.6
  153.3 5.7 convolution_convert_fusion.1
  160.2 3.8 collective-permute-start
  164.0 2.1 collective-permute-start.1
  168.4 2.1 fusion.44
  170.6 2.1 pad_maximum_fusion.3
  174.5 17.0 %all-gather.14.cloned.1.call-done = bf16[2048,256]{1,0:T(8,128)(2,1)} async-done(((bf16[128,256]{1,0:T(8,128)(2,1)}), bf16[2048,256]{1,0:T(8,128)(2,1)}) %all-gather.14.cloned.1.call-update) | async-done | bytes 1048592 | tf_op jit(solution)/shard_map/all_gather | solution.py:135
  191.5 45.9 %all-gather.16.cloned.1.call-done = bf16[2048,256]{1,0:T(8,128)(2,1)} async-done(((bf16[128,256]{1,0:T(8,128)(2,1)}), bf16[2048,256]{1,0:T(8,128)(2,1)}) %all-gather.16.cloned.1.call-update) | async-done | bytes 1048592 | tf_op jit(solution)/shard_map/all_gather | solution.py:136
  239.1 66.2 %gather_fusion = bf16[16384,512]{1,0:T(8,128)(2,1)} fusion(bf16[2048,512]{1,0:T(8,128)(2,1)S(1)} %pad_maximum_fusion, s32[16384]{0:T(1024)S(1)} %broadcast_clamp_fusion), kind=kCustom, calls=%fused_computation | custom fusion | bytes 33619968 | tf_op jit(solution)/shard_map/gather | solution.py:33
  305.3 7.5 fusion
  312.7 2.4 broadcast_divide_fusion
  315.1 111.0 %all-gather.20.cloned.1.call-done = bf16[65536,256]{1,0:T(8,128)(2,1)} async-done(((bf16[4096,256]{1,0:T(8,128)(2,1)}), bf16[65536,256]{1,0:T(8,128)(2,1)}) %all-gather.20.cloned.1.call-update) | async-done | bytes 33554448 | tf_op jit(solution)/shard_map/all_gather | solution.py:164
  426.1 11.6 %reduce_sum.42 = bf16[4096,256]{1,0:T(8,128)(2,1)S(1)} reduce(bf16[16,4096,256]{2,1,0:T(8,128)(2,1)} %bitcast.104, bf16[]{:T(256)} %constant.71.clone.1), dimensions={0}, to_apply=%region_0.0 | reduce | flops 15728640 | bytes 35651584 | tf_op jit(solution)/shard_map/reduce_sum | solution.py:164
  439.4 2.8 bitcast_add_fusion
  443.8 3.4 fusion.15
  447.3 88.8 %all-gather.18.cloned.1.call-done = bf16[16384,256]{1,0:T(8,128)(2,1)} async-done(((bf16[2048,256]{1,0:T(8,128)(2,1)}), bf16[16384,256]{1,0:T(8,128)(2,1)}) %all-gather.18.cloned.1.call-update) | async-done | bytes 8388624 | tf_op jit(solution)/shard_map/all_gather | solution.py:161
  536.1 4.8 convolution_convert_fusion.2
  540.9 9.6 %convolution_convert_fusion = bf16[4096,256]{1,0:T(8,128)(2,1)} fusion(bf16[4096,2048]{1,0:T(8,128)(2,1)} %bitcast.110, bf16[2048,256]{1,0:T(8,128)(2,1)S(1)} %bitcast.124), kind=kOutput, calls=%fused_computation.7 | convolution fusion | flops 4296015872 | bytes 19922944 | tf_op jit(solution)/shard_map/dot_general | solution.py:163
  551.8 3.8 collective-permute-start.2
  555.7 2.1 collective-permute-start.3
  557.8 3.1 fusion.47
  564.9 172.4 %all-gather.22.cloned.1.call-done = bf16[65536,256]{1,0:T(8,128)(2,1)} async-done(((bf16[4096,256]{1,0:T(8,128)(2,1)}), bf16[65536,256]{1,0:T(8,128)(2,1)}) %all-gather.22.cloned.1.call-update) | async-done | bytes 33554448 | tf_op jit(solution)/shard_map/all_gather | solution.py:164
  737.3 13.0 %reduce_sum.45 = bf16[4096,256]{1,0:T(8,128)(2,1)} reduce(bf16[16,4096,256]{2,1,0:T(8,128)(2,1)} %bitcast.105, bf16[]{:T(256)} %constant.71.clone.1), dimensions={0}, to_apply=%region_3.4 | reduce | flops 15728640 | bytes 35651584 | tf_op jit(solution)/shard_map/reduce_sum | solution.py:164
  751.9 2.9 add_add_fusion
  756.6 4.3 multiply_add_fusion
  (103 shorter events, 24.4 us)
Async XLA Ops:
  7.2 76.7 %all-gather.10.cloned.1.call-start = ((), (), s32[]{:S(2)}) async-start(), calls=%async_computation | async-start | bytes 1179648 | tf_op jit(solution)/shard_map/all_gather | solution.py:157
  7.9 4.6 copy-start.25
  7.9 136.9 %all-gather.12.cloned.1.call-start = ((), (), s32[]{:S(2)}) async-start(), calls=%async_computation.1 | async-start | bytes 9437184 | tf_op jit(solution)/shard_map/all_gather | solution.py:161
  10.6 180.9 %all-gather.14.cloned.1.call-start = ((), (), s32[]{:S(2)}) async-start(), calls=%async_computation.2 | async-start | bytes 1114112 | tf_op jit(solution)/shard_map/all_gather | solution.py:135
  11.4 226.0 %all-gather.16.cloned.1.call-start = ((), (), s32[]{:S(2)}) async-start(), calls=%async_computation.3 | async-start | bytes 1114112 | tf_op jit(solution)/shard_map/all_gather | solution.py:136
  12.0 414.2 %all-gather.20.cloned.1.call-start = ((), (), s32[]{:S(2)}) async-start(), calls=%async_computation.5 | async-start | bytes 35651584 | tf_op jit(solution)/shard_map/all_gather | solution.py:164
  144.8 8.5 %copy-start.6 = (bf16[512,8,8,256]{3,1,2,0:T(8,128)(2,1)S(1)}, bf16[512,8,8,256]{3,1,2,0:T(8,128)(2,1)}, u32[]{:S(2)}) copy-start(bf16[512,8,8,256]{3,1,2,0:T(8,128)(2,1)} %copy.31) | copy-start | bytes 50331652
  159.0 7.2 copy-start.18
  159.0 377.1 %all-gather.18.cloned.1.call-start = ((), (), s32[]{:S(2)}) async-start(), calls=%async_computation.4 | async-start | bytes 9437184 | tf_op jit(solution)/shard_map/all_gather | solution.py:161
  160.2 10.4 %collective-permute-start = (bf16[256,256]{1,0:T(8,128)(2,1)S(1)}, bf16[256,256]{1,0:T(8,128)(2,1)}, u32[]{:S(2)}, u32[]{:S(2)}) collective-permute-start(bf16[256,256]{1,0:T(8,128)(2,1)S(1)} %get-tuple-element.18), channel_id=1, source_target_pairs={{0,1},{1,2},{2,3},{3,4},{4,5},{5,6},{6,7},{7,8},{8,9},{9,10},{10,1... | collective-permute-start | bytes 393224 | tf_op jit(solution)/shard_map/ppermute | solution.py:20
  164.0 6.6 collective-permute-start.1
  168.3 2.1 copy-start.12
  168.3 4.4 copy-start.10
  168.3 270.0 %copy-start.8 = (bf16[1,2048,256]{2,1,0:T(8,128)(2,1)}, bf16[1,2048,256]{2,1,0:T(8,128)(2,1)S(1)}, u32[]{:S(2)}) copy-start(bf16[1,2048,256]{2,1,0:T(8,128)(2,1)S(1)} %get-tuple-element.8) | copy-start | bytes 3145732
  168.3 2.2 copy-start.19
  168.4 2.2 copy-start.26
  426.1 11.7 %copy-start.17 = (bf16[32,2048]{1,0:T(8,128)(2,1)S(1)}, bf16[32,2048]{1,0:T(8,128)(2,1)}, u32[]{:S(2)}) copy-start(bf16[32,2048]{1,0:T(8,128)(2,1)} %param.28) | copy-start | bytes 393220
  439.4 2.8 copy-start
  439.4 3.8 copy-start.1
  439.4 4.4 copy-start.14
  439.4 4.4 copy-start.21
  439.4 4.4 copy-start.22
  439.4 4.4 copy-start.23
  439.4 4.4 copy-start.24
  447.2 88.9 %copy-start.7 = (bf16[32,16384]{1,0:T(8,128)(2,1)S(1)}, bf16[32,16384]{1,0:T(8,128)(2,1)}, u32[]{:S(2)}) copy-start(bf16[32,16384]{1,0:T(8,128)(2,1)} %all-gather.10.cloned.1.call-done) | copy-start | bytes 3145732
  447.2 290.1 %all-gather.22.cloned.1.call-start = ((), (), s32[]{:S(2)}) async-start(), calls=%async_computation.6 | async-start | bytes 35651584 | tf_op jit(solution)/shard_map/all_gather | solution.py:164
  551.8 9.0 %collective-permute-start.2 = (bf16[256,256]{1,0:T(8,128)(2,1)S(1)}, bf16[256,256]{1,0:T(8,128)(2,1)S(1)}, u32[]{:S(2)}, u32[]{:S(2)}) collective-permute-start(bf16[256,256]{1,0:T(8,128)(2,1)S(1)} %get-tuple-element.13), channel_id=1, source_target_pairs={{0,1},{1,2},{2,3},{3,4},{4,5},{5,6},{6,7},{7,8},{8,9},{9,10},{10,1... | collective-permute-start | bytes 393224 | tf_op jit(solution)/shard_map/ppermute | solution.py:20
  555.7 6.3 collective-permute-start.3
  560.9 2.2 copy-start.11
  751.9 3.4 copy-start.2
  751.9 4.1 copy-start.5
  751.9 4.7 copy-start.15
  (7 other events, 8.6 us)
Sparse Core Ops, SparseCore 0:
  9.6 36.8 all-gather.9
  48.8 95.9 all-gather.11
  147.3 44.2 all-gather.13
  193.8 43.5 all-gather.15
  240.3 185.8 all-gather.19
  447.4 88.6 all-gather.17
  550.7 186.5 all-gather.21
